TPU v7x, 256 devices: a whole 4x4x8 slice. The times are simulated.
256 devices in a mesh: box: 64 (over y, x, z_lo, core), dir: 4 (over z_hi).
Axes of the slice: x: 4, y: 4, z: 8 (z_hi: 4, z_lo: 2; z = z_hi * 2 + z_lo), core: 2. Of those that a mesh axis runs over, the one named last changes fastest.
Arguments:
- child_field: float32 [2, 4, 2048, 4608], P(None, None, 'box', 'dir'), may hold values from -6 to 6
- child_of: int32 [512, 4], P('box'), may hold values from 0 to 2047, as said below
- shift_angle: float32 [4, 18432], P(None, 'dir'), may hold values from -3.140625 to 3.140625
- interp_index: int32 [6, 18432], P(None, 'dir'), may hold values from 0 to 4607, as said below
- interp_weight: float32 [6, 18432], P(None, 'dir'), may hold values from -0.2 to 0.5
- interaction_list: int32 [27, 512], replicated, may hold values from 0 to 511
- translation: float32 [2, 27, 18432], P(None, None, 'dir'), may hold values from -0.875 to 0.875
Outputs:
- child_incoming: float32 [2, 4, 2048, 4608], P(None, None, 'box', 'dir')
Inputs may be any that keep to these rules, and one draw needn't show every extreme that they name: child_of lists every child box once; the parents p with p // 8 = q have exactly the children q * 32 to (q + 1) * 32 - 1. interp_index[j, k] differs from k // 4 by at most 8, and for j = 0 by exactly 8 where k // 4 lies 8 or more from both ends.
All inputs are finite; a program needn't handle non-finite values.
Results may differ from a plain program's by a relative error of at most 0.00007.
Values sent between devices are 32-bit elements; how exact they have to be, the bound alone decides.
No kernel may reach another device: no remote copies, remote signals or barrier semaphores. Data moves between devices by JAX's collectives and lax.ppermute only.
A program may use at most 64 MiB of HBM per device.

v0:
```python
import jax
import jax.numpy as jnp
from jax import lax
from jax.sharding import PartitionSpec as P

KIDS = 4
HW = 8


def padded(block, sides, width):
    for axis, dim in sides:
        count = lax.axis_size(axis)
        forward = [(i, i + 1) for i in range(count - 1)]
        backward = [(target, source) for source, target in forward]
        low = lax.ppermute(
            lax.slice_in_dim(block, block.shape[dim] - width, None, axis=dim), axis, forward
        )
        high = lax.ppermute(lax.slice_in_dim(block, 0, width, axis=dim), axis, backward)
        block = jnp.concatenate([low, block, high], axis=dim)
    return block


def from_behind(block, axis, distance):
    devices = range(lax.axis_size(axis))
    route = [(i - distance, i) for i in devices if i - distance in devices]
    return lax.ppermute(block, axis, route)


def translate(source_field, interaction_list, table):

    def add_term(term, carry):
        source_ids = lax.dynamic_index_in_dim(interaction_list, term, 0, keepdims=False)
        source = jnp.take(source_field, source_ids, axis=0)
        op_real = lax.dynamic_index_in_dim(table[0], term, 0, keepdims=False)
        op_imag = lax.dynamic_index_in_dim(table[1], term, 0, keepdims=False)
        src_real = source[:, 0]
        src_imag = source[:, 1]
        return (
            carry[0] + op_real * src_real - op_imag * src_imag,
            carry[1] + op_real * src_imag + op_imag * src_real,
        )

    start = jnp.zeros(source_field[:, 0].shape, jnp.float32)
    real_sum, imag_sum = lax.fori_loop(0, interaction_list.shape[0], add_term, (start, start))
    return jnp.stack([real_sum, imag_sum], axis=1)


def shards(
    child_field, child_of, shift_angle, interp_index, interp_weight, interaction_list, translation
):
    box_count = lax.axis_size("box")
    box_index = lax.axis_index("box")
    dir_index = lax.axis_index("dir")
    halves, fields, own_boxes, strip_child = child_field.shape
    parents = child_of.shape[0]
    strip_par = interp_index.shape[1]
    dir_piece = strip_par // box_count
    block_len = 512
    block_count = strip_par // block_len
    window = block_len // 4 + 2 * HW
    row_count = halves * fields * own_boxes

    def build_matrix(block_at):
        index_block = lax.dynamic_slice_in_dim(interp_index, block_at * block_len, block_len, 1)
        weight_block = lax.dynamic_slice_in_dim(interp_weight, block_at * block_len, block_len, 1)
        columns = index_block - dir_index * strip_child + HW - block_at * (block_len // 4)
        places = lax.iota(jnp.int32, window)[:, None]
        matrix = jnp.zeros((window, block_len), jnp.float32)
        for stencil_at in range(index_block.shape[0]):
            matrix = matrix + jnp.where(
                columns[stencil_at][None, :] == places, weight_block[stencil_at][None, :], 0.0
            )
        return matrix

    matrices = lax.map(build_matrix, jnp.arange(block_count, dtype=jnp.int32))
    extended = padded(child_field, (("dir", 3),), HW)
    flattened = extended.reshape(row_count, strip_child + 2 * HW)

    def interp_block(block_at, summed):
        columns = lax.dynamic_slice_in_dim(flattened, block_at * (block_len // 4), window, 1)
        product = jnp.dot(
            columns,
            matrices[block_at],
            precision=lax.Precision.HIGHEST,
            preferred_element_type=jnp.float32,
        )
        return lax.dynamic_update_slice_in_dim(summed, product, block_at * block_len, 1)

    interpolated = lax.fori_loop(
        0, block_count, interp_block, jnp.zeros((row_count, strip_par), jnp.float32)
    )
    interpolated = interpolated.reshape(halves, fields, own_boxes, strip_par)
    local_kids = (child_of - box_index * own_boxes).reshape(-1)
    selector = (local_kids[:, None] == lax.iota(jnp.int32, own_boxes)[None, :]).astype(jnp.float32)
    picked = jnp.einsum(
        "qb,crbn->qcrn",
        selector,
        interpolated,
        precision=lax.Precision.HIGHEST,
        preferred_element_type=jnp.float32,
    )
    picked = picked.reshape(parents, KIDS, halves, fields, strip_par)
    cosines = jnp.cos(shift_angle)[None, :, None, :]
    sine_part = jnp.sin(shift_angle)[None, :, None, :]
    agg_real = jnp.sum(picked[:, :, 0] * cosines - picked[:, :, 1] * sine_part, axis=1)
    agg_imag = jnp.sum(picked[:, :, 0] * sine_part + picked[:, :, 1] * cosines, axis=1)
    aggregated = jnp.stack([agg_real, agg_imag], axis=1)
    outbound = aggregated.reshape(parents, halves, fields, box_count, dir_piece)
    table = lax.dynamic_slice_in_dim(translation, box_index * dir_piece, dir_piece, 2)
    received = lax.all_to_all(outbound, "box", split_axis=3, concat_axis=0, tiled=True)
    answered = translate(received[:, :, :, 0], interaction_list, table)
    incoming = lax.all_to_all(
        answered[:, :, :, None], "box", split_axis=0, concat_axis=3, tiled=True
    )
    incoming = incoming.reshape(parents, halves, fields, strip_par)
    in_real = incoming[:, 0][:, None]
    in_imag = incoming[:, 1][:, None]
    spread_real = in_real * cosines + in_imag * sine_part
    spread_imag = in_imag * cosines - in_real * sine_part
    spread_kids = jnp.stack([spread_real, spread_imag], axis=2).reshape(
        parents * KIDS, halves, fields, strip_par
    )
    spread = jnp.einsum(
        "qb,qcrn->crbn",
        selector,
        spread_kids,
        precision=lax.Precision.HIGHEST,
        preferred_element_type=jnp.float32,
    ).reshape(row_count, strip_par)

    def anterp_block(block_at, summed):
        columns = lax.dynamic_slice_in_dim(spread, block_at * block_len, block_len, 1)
        product = jnp.dot(
            columns,
            matrices[block_at].T,
            precision=lax.Precision.HIGHEST,
            preferred_element_type=jnp.float32,
        )
        current = lax.dynamic_slice_in_dim(summed, block_at * (block_len // 4), window, 1)
        return lax.dynamic_update_slice_in_dim(
            summed, current + product, block_at * (block_len // 4), 1
        )

    widened = lax.fori_loop(
        0, block_count, anterp_block, jnp.zeros((row_count, strip_child + 2 * HW), jnp.float32)
    )
    widened = widened.reshape(halves, fields, own_boxes, strip_child + 2 * HW)
    inner = widened[..., HW : HW + strip_child]
    from_below = from_behind(widened[..., strip_child + HW :], "dir", 1)
    from_above = from_behind(widened[..., :HW], "dir", -1)
    return inner.at[..., :HW].add(from_below).at[..., strip_child - HW :].add(from_above)


def solution(mesh):
    in_specs = (
        P(None, None, "box", "dir"),
        P("box", None),
        P(None, "dir"),
        P(None, "dir"),
        P(None, "dir"),
        P(),
        P(None, None, "dir"),
    )
    out_specs = P(None, None, "box", "dir")
    return jax.shard_map(shards, mesh=mesh, in_specs=in_specs, out_specs=out_specs, check_vma=False)
```

profile of v0, /device:TPU:65, one launch (start us, length us, event | category | flops | bytes accessed | tf_op | source)
XLA Modules:
  0.0 551.9 jit_solution(9596566459569642869)
XLA Ops:
  1.2 6.1 %collective-permute-start = (f32[2,4,32,8]{3,2,1,0:T(8,128)S(1)}, f32[2,4,32,8]{3,2,1,0:T(8,128)S(1)}, u32[]{:S(2)}, u32[]{:S(2)}) collective-permute-start(f32[2,4,32,8]{3,2,1,0:T(8,128)S(1)} %get-tuple-element.476), channel_id=1, source_target_pairs={{0,1},{1,2},{2,3},{4,5},{5,6},{6,7},{8,9},{9,10},{10,11},{12,13},{... | collective-permute-start | bytes 24584 | tf_op jit(solution)/shard_map/ppermute | solution.py:15
  9.3 39.6 %while.56 = (s32[]{:T(128)}, f32[9,144,512]{2,1,0:T(8,128)}, s32[9]{0:T(128)S(1)}, s32[6,4608]{1,0:T(8,128)}, s32[]{:T(128)}, /*index=5*/f32[6,4608]{1,0:T(8,128...) while((s32[]{:T(128)}, f32[9,144,512]{2,1,0:T(8,128)}, ...), condition=%wide.region_1.2_spmd, body=%wide.region_0.1_spmd.sunk | while | flops 1262604 | bytes 394043 | solution.py:75
  55.9 21.4 %while.57 = (s32[]{:T(128)}, f32[256,4608]{1,0:T(8,128)}, f32[256,1168]{1,0:T(8,128)S(1)}, f32[9,144,512]{2,1,0:T(8,128)}, s32[]{:T(128)}, /*index=5*/s32[]{:T(128)}, s32[]{:T(128)}, s32[]{:T(128)}, s32[]{:T(128)}, s32[]{:T(128)}) while((s32[]{:T(128)}, f32[256,4608]{1,0:T(8,128)}, f32[256,1168]{1,0:T(8,128)S(1)}, f32[9,144,512]{2,1,0:T(8,128)}, ...), condition=%wide.region_3.4_spmd, body=%wide.region_2.3_spmd.sunk | while | flops 226492432 | bytes 1082057 | solution.py:89
  77.3 4.8 fusion.18
  89.6 8.9 %all-to-all-start = ((f32[8,2,4,64,72]{4,0,2,1,3:T(8,128)}), f32[8,2,4,64,72]{4,0,2,1,3:T(8,128)S(1)}, u32[]{:S(2)}, u32[]{:S(2)}) async-start(f32[8,2,4,64,72]{4,0,2,1,3:T(8,128)} %copy.29), calls=%async_computation | async-start | bytes 4194304 | tf_op jit(solution)/shard_map/all_to_all | solution.py:110
  98.7 29.4 %all-to-all-done = f32[8,2,4,64,72]{4,0,2,1,3:T(8,128)S(1)} async-done(((f32[8,2,4,64,72]{4,0,2,1,3:T(8,128)}), f32[8,2,4,64,72]{4,0,2,1,3:T(8,128)S(1)}, u32[]{:S(2)}, u32[]{:S(2)}) %all-to-all-start) | async-done | bytes 1179680 | tf_op jit(solution)/shard_map/all_to_all | solution.py:110
  130.9 326.6 %while.59 = (s32[]{:T(128)}, f32[512,4,72]{2,1,0:T(4,128)}, f32[512,4,72]{2,1,0:T(4,128)}, f32[2,27,72]{2,1,0:T(8,128)S(1)}, s32[27,512]{1,0:T(8,128)}, /*index=5*/f32[512,2,4,72]{3,2,1,0:T(4,128)}, s32[]{:T(128)}, s32[]{:T(128)}) while((s32[]{:T(128)}, f32[512,4,72]{2,1,0:T(4,128)}, f32[512,4,72]{2,1,0:T(4,128)}, ...), condition=%wide.region_7.8_spmd.clone, body=%wide.region_6.7_spmd.clone.sunk | while | flops 1775107 | bytes 8307879 | solution.py:44
  131.7 4.9 gather_fusion
  142.3 4.9 gather_fusion
  154.4 4.9 gather_fusion
  162.2 3.6 fusion.49
  166.6 4.9 gather_fusion
  178.7 4.9 gather_fusion
  190.9 4.9 gather_fusion
  203.0 4.9 gather_fusion
  215.2 4.9 gather_fusion
  223.0 3.6 fusion.49
  227.3 4.9 gather_fusion
  239.5 4.9 gather_fusion
  247.3 3.6 fusion.49
  251.6 4.9 gather_fusion
  259.4 3.6 fusion.49
  263.8 4.9 gather_fusion
  271.6 3.6 fusion.49
  275.9 4.9 gather_fusion
  288.1 4.9 gather_fusion
  300.3 4.9 gather_fusion
  308.0 3.6 fusion.49
  312.4 4.9 gather_fusion
  324.6 4.9 gather_fusion
  336.7 4.9 gather_fusion
  348.9 4.9 gather_fusion
  356.7 3.6 fusion.49
  361.0 4.9 gather_fusion
  373.2 4.9 gather_fusion
  385.3 4.9 gather_fusion
  397.5 4.9 gather_fusion
  409.6 4.9 gather_fusion
  421.8 4.9 gather_fusion
  429.6 3.6 fusion.49
  433.9 4.9 gather_fusion
  446.1 4.9 gather_fusion
  460.9 4.6 all-to-all-start.1
  467.9 27.2 %all-to-all-done.1 = f32[512,2,4,1,72]{4,2,1,3,0:T(4,128)S(1)} async-done(((f32[512,2,4,1,72]{4,2,1,3,0:T(4,128)}), f32[512,2,4,1,72]{4,2,1,3,0:T(4,128)S(1)}, u32[]{:S(2)}, u32[]{:S(2)}) %all-to-all-start.1) | async-done | bytes 1179680 | tf_op jit(solution)/shard_map/all_to_all | solution.py:112
  508.2 4.8 fusion.13
  513.1 16.5 %while.58 = (s32[]{:T(128)}, f32[256,1168]{0,1:T(8,128)S(1)}, f32[256,4608]{1,0:T(8,128)}, f32[9,144,512]{2,1,0:T(8,128)}, s32[]{:T(128)}, /*index=5*/s32[]{:T(128)}, s32[]{:T(128)}, s32[]{:T(128)}, s32[]{:T(128)}, s32[]{:T(128)}) while((s32[]{:T(128)}, f32[256,1168]{0,1:T(8,128)S(1)}, f32[256,4608]{1,0:T(8,128)}, f32[9,144,512]{2,1,0:T(8,128)}, ...), condition=%wide.region_9.10_spmd, body=%wide.region_8.9_spmd.sunk | while | flops 226529296 | bytes 1114825 | solution.py:144
  530.7 5.7 %collective-permute-start.2 = (f32[2,4,32,8]{3,2,1,0:T(8,128)S(1)}, f32[2,4,32,8]{3,2,1,0:T(8,128)S(1)}, u32[]{:S(2)}, u32[]{:S(2)}) collective-permute-start(f32[2,4,32,8]{3,2,1,0:T(8,128)S(1)} %get-tuple-element.472), channel_id=1, source_target_pairs={{0,1},{1,2},{2,3},{4,5},{5,6},{6,7},{8,9},{9,10},{10,11},{12,13},{... | collective-permute-start | bytes 24584 | tf_op jit(solution)/shard_map/ppermute | solution.py:26
  541.7 6.9 %collective-permute-done.3 = f32[2,4,32,8]{3,2,1,0:T(8,128)} collective-permute-done((f32[2,4,32,8]{3,2,1,0:T(8,128)}, f32[2,4,32,8]{3,2,1,0:T(8,128)}, u32[]{:S(2)}, u32[]{:S(2)}) %collective-permute-start.3) | collective-permute-done | bytes 8224 | tf_op jit(solution)/shard_map/ppermute | solution.py:26
  (308 shorter events, 281.4 us)
Async XLA Ops:
  0.0 98.6 %copy-start = (f32[2,27,4608]{2,0,1:T(2,128)S(1)}, f32[2,27,4608]{2,0,1:T(2,128)}, u32[]{:S(2)}) copy-start(f32[2,27,4608]{2,0,1:T(2,128)} %param.25) | copy-start | bytes 2985988
  0.0 51.7 %copy-start.3 = (f32[2,4,32,1152]{3,2,1,0:T(8,128)S(1)}, f32[2,4,32,1152]{3,2,1,0:T(8,128)}, u32[]{:S(2)}) copy-start(f32[2,4,32,1152]{3,2,1,0:T(8,128)} %param.19) | copy-start | bytes 3538948
  0.0 51.0 %copy-start.8 = (s32[8,4]{0,1:T(4,128)S(1)}, s32[8,4]{0,1:T(4,128)}, u32[]{:S(2)}) copy-start(s32[8,4]{0,1:T(4,128)} %param.20) | copy-start | bytes 388
  1.2 49.8 %collective-permute-start = (f32[2,4,32,8]{3,2,1,0:T(8,128)S(1)}, f32[2,4,32,8]{3,2,1,0:T(8,128)S(1)}, u32[]{:S(2)}, u32[]{:S(2)}) collective-permute-start(f32[2,4,32,8]{3,2,1,0:T(8,128)S(1)} %get-tuple-element.476), channel_id=1, source_target_pairs={{0,1},{1,2},{2,3},{4,5},{5,6},{6,7},{8,9},{9,10},{10,11},{12,13},{... | collective-permute-start | bytes 24584 | tf_op jit(solution)/shard_map/ppermute | solution.py:15
  7.4 44.3 %collective-permute-start.1 = (f32[2,4,32,8]{3,2,1,0:T(8,128)S(1)}, f32[2,4,32,8]{3,2,1,0:T(8,128)}, u32[]{:S(2)}, u32[]{:S(2)}) collective-permute-start(f32[2,4,32,8]{3,2,1,0:T(8,128)S(1)} %get-tuple-element.475), channel_id=1, source_target_pairs={{1,0},{2,1},{3,2},{5,4},{6,5},{7,6},{9,8},{10,9},{11,10},{13,12},{... | collective-permute-start | bytes 24584 | tf_op jit(solution)/shard_map/ppermute | solution.py:18
  51.0 0.7 copy-start.7
  77.3 4.8 copy-start.5
  77.3 4.8 copy-start.6
  89.6 38.5 %all-to-all-start = ((f32[8,2,4,64,72]{4,0,2,1,3:T(8,128)}), f32[8,2,4,64,72]{4,0,2,1,3:T(8,128)S(1)}, u32[]{:S(2)}, u32[]{:S(2)}) async-start(f32[8,2,4,64,72]{4,0,2,1,3:T(8,128)} %copy.29), calls=%async_computation | async-start | bytes 4194304 | tf_op jit(solution)/shard_map/all_to_all | solution.py:110
  460.9 34.2 %all-to-all-start.1 = ((f32[512,2,4,1,72]{4,2,1,3,0:T(4,128)}), f32[512,2,4,1,72]{4,2,1,3,0:T(4,128)S(1)}, u32[]{:S(2)}, u32[]{:S(2)}) async-start(f32[512,2,4,1,72]{4,2,1,3,0:T(4,128)} %maximum_bitcast_fusion), calls=%async_computation.1 | async-start | bytes 4194304 | tf_op jit(solution)/shard_map/all_to_all | solution.py:112
  503.2 1.9 copy-start.2
  529.6 22.1 %copy-start.1 = (f32[2,27,4608]{2,0,1:T(2,128)S(1)}, f32[2,27,4608]{2,0,1:T(2,128)}, u32[]{:S(2)}) copy-start(f32[2,27,4608]{2,0,1:T(2,128)} %param.25) | copy-start | bytes 2985988
  530.7 9.0 %collective-permute-start.2 = (f32[2,4,32,8]{3,2,1,0:T(8,128)S(1)}, f32[2,4,32,8]{3,2,1,0:T(8,128)S(1)}, u32[]{:S(2)}, u32[]{:S(2)}) collective-permute-start(f32[2,4,32,8]{3,2,1,0:T(8,128)S(1)} %get-tuple-element.472), channel_id=1, source_target_pairs={{0,1},{1,2},{2,3},{4,5},{5,6},{6,7},{8,9},{9,10},{10,11},{12,13},{... | collective-permute-start | bytes 24584 | tf_op jit(solution)/shard_map/ppermute | solution.py:26
  536.8 11.7 %collective-permute-start.3 = (f32[2,4,32,8]{3,2,1,0:T(8,128)}, f32[2,4,32,8]{3,2,1,0:T(8,128)}, u32[]{:S(2)}, u32[]{:S(2)}) collective-permute-start(f32[2,4,32,8]{3,2,1,0:T(8,128)} %get-tuple-element.471), channel_id=1, source_target_pairs={{1,0},{2,1},{3,2},{5,4},{6,5},{7,6},{9,8},{10,9},{11,10},{13,12},{... | collective-permute-start | bytes 24584 | tf_op jit(solution)/shard_map/ppermute | solution.py:26
  541.6 7.9 %copy-start.4 = (f32[2,4,32,1152]{3,2,1,0:T(8,128)}, f32[2,4,32,1152]{3,2,1,0:T(8,128)S(1)}, u32[]{:S(2)}) copy-start(f32[2,4,32,1152]{3,2,1,0:T(8,128)S(1)} %scatter-add.6) | copy-start | bytes 3538948
where the time goes:
time: 558 us; the launch traced here: 552 us
  other arithmetic  219 us (39%)
  local copies, waits for them, and re-layouts  180 us (32%)
  waiting for transfers between devices  64.5 us (12%)
  matrix products  47.2 us (8%)
  starting transfers between devices  29.2 us (5%)
  loops' own time  11.3 us (2%)
    gather x27, local copies, waits for them, and re-layouts, add_term(): source = jnp.take(source_field, source_ids, axis=0)  131 us
    select_n x54, other arithmetic, add_term(): source = jnp.take(source_field, source_ids, axis=0)  97.4 us
    add x27, other arithmetic, add_term(): carry[1] + op_real * src_imag + op_imag * src_real  96.2 us
    all_to_all x1, waiting for transfers between devices, shards(): lax.all_to_all(outbound, 'box', split_axis=3, concat_axis=0, tiled=True)  29.4 us
    all_to_all x1, waiting for transfers between devices, shards(): lax.all_to_all(answered[:, :, :, None], 'box', split_axis=0, concat_axis=...  27.2 us
    dot_general x9, matrix products, interp_block(): jnp.dot(columns, matrices[block_at], precision=lax.Precision.HIGHEST, pre...  21.4 us
    dot_general x9, matrix products, anterp_block(): jnp.dot(columns, matrices[block_at].T, precision=lax.Precision.HIGHEST, p...  16.3 us
  transfers between devices with their start and end apart: 6, of which 4 were waited for; matrix products, arithmetic and copies ran while one was open for 7% of the time, Pallas kernels for 0%

commit v1 on v0

v1 whole, which is shorter than its diff:
```python
import jax
import jax.numpy as jnp
from jax import lax
from jax.experimental import pallas as pl
from jax.experimental.pallas import tpu as pltpu
from jax.sharding import PartitionSpec as P

F32 = jnp.float32
BF16 = jnp.bfloat16
HW = 8
KIDS = 4
PAR = 8
TERMS = 27
STENCIL = 6
EXTRA = 16
MAIN = 64
PACK_ROWS = 120
IDX_AT, WEIGHT_AT, SHIFT_AT, REAL_AT, IMAG_AT = 32, 40, 48, 56, 88


def lanes(shape=(8, 128)):
    return lax.broadcasted_iota(jnp.int32, shape, 1)


def rows(shape=(8, 128)):
    return lax.broadcasted_iota(jnp.int32, shape, 0)


def turn(value, shift):
    shift = shift % 128
    return value if shift == 0 else pltpu.roll(value, shift, 1)


def kid_rows(kids_ref, at):
    s, p = at // PAR, at % PAR
    return pl.ds(kids_ref[p * KIDS + s] % 32, 8, stride=32)


def split(value):
    high = value.astype(BF16)
    return high, (value - high.astype(F32)).astype(BF16)


def stencil_matrix(columns, weights, width, used):
    parts = []
    for group in range(used // 8):
        places = rows((8, width)) + 8 * group
        summed = jnp.zeros((8, width), F32)
        for j in range(STENCIL):
            summed = summed + jnp.where(columns[j : j + 1, :] == places, weights[j : j + 1, :], 0.0)
        parts.append(summed)
    parts.append(jnp.zeros((128 - used, width), F32))
    return split(jnp.concatenate(parts, axis=0))


def interp_product(tile, matrix):
    high, low = split(tile)
    both = jnp.concatenate([high, high], axis=1)
    return jnp.dot(both, matrix, preferred_element_type=F32) + jnp.dot(
        low, matrix[:128], preferred_element_type=F32
    )


def anterp_product(spread, matrix):
    high, low = split(spread)
    dims = (((1,), (1,)), ((), ()))
    first = lax.dot_general(high, matrix, dims, preferred_element_type=F32)
    second = lax.dot_general(low, matrix[:128], dims, preferred_element_type=F32)
    return first[:, :128] + first[:, 128:] + second


def swapped(value):
    return pltpu.roll(value, 4, 0)


def sign(width):
    return jnp.where(rows((8, width)) < 4, -1.0, 1.0).astype(F32)


def aggregate(product, cosines, sines):
    width = product.shape[1]
    flip = sign(width)
    out = []
    for p in range(PAR):
        straight = jnp.zeros((8, width), F32)
        crossed = jnp.zeros((8, width), F32)
        for s in range(KIDS):
            piece = product[(s * PAR + p) * 8 : (s * PAR + p) * 8 + 8, :]
            straight = straight + piece * cosines[s : s + 1, :]
            crossed = crossed + piece * sines[s : s + 1, :]
        out.append(straight + flip * swapped(crossed))
    return out


def send_main(out_tiles, store):
    low = lanes() < MAIN
    for q in range(PAR // 2):
        first, second = out_tiles[2 * q], out_tiles[2 * q + 1]
        store(0, q, jnp.where(low, first, turn(second, MAIN)))
        store(1, q, jnp.where(low, turn(first, MAIN), second))


def pack_kernel(kids, child_lo, child_hi, idx_lo, idx_hi, w_lo, w_hi, a_lo, a_hi, t_lo, t_hi, lo_ref, hi_ref):
    piece = lanes() // EXTRA
    for a in range(KIDS):
        low_tile = jnp.zeros((8, 128), F32)
        high_tile = jnp.zeros((8, 128), F32)
        for i in range(8):
            at = kid_rows(kids, 8 * a + i)
            low_tile = jnp.where(piece == i, turn(child_lo[at, :], 16 * i), low_tile)
            high_tile = jnp.where(piece == i, turn(child_hi[at, :], 16 * i + 16), high_tile)
        lo_ref[8 * a : 8 * a + 8, :] = low_tile
        hi_ref[8 * a : 8 * a + 8, :] = high_tile
    for ref, idx, w, a, t in ((lo_ref, idx_lo, w_lo, a_lo, t_lo), (hi_ref, idx_hi, w_hi, a_hi, t_hi)):
        ref[32:, :] = jnp.zeros((PACK_ROWS - 32, 128), F32)
        ref[IDX_AT : IDX_AT + STENCIL, :] = idx[...].astype(F32)
        ref[WEIGHT_AT : WEIGHT_AT + STENCIL, :] = w[...]
        ref[SHIFT_AT : SHIFT_AT + KIDS, :] = a[...]
        ref[REAL_AT : REAL_AT + TERMS, :] = t[0]
        ref[IMAG_AT : IMAG_AT + TERMS, :] = t[1]


def inner_kernel(kids, where, child, idx, weight, angle, send, matrices, phases, ends, raw, own, sems):
    base = where[1] * child.shape[1]
    count = child.shape[1] // 128
    copies = [
        pltpu.make_async_copy(child.at[:, 128 * t : 128 * t + 128], raw.at[t], sems.at[t])
        for t in range(count)
    ]
    for copy in copies:
        copy.start()
    for t in range(count):
        copies[t].wait()
        for at in range(PAR * KIDS):
            own[t, 8 * at : 8 * at + 8, :] = raw.at[t][kid_rows(kids, at), :]
    ends[0] = own[0]
    ends[1] = own[count - 2]
    ends[2] = own[count - 1]

    def fill_matrix(block):
        cut = pl.ds(pl.multiple_of(block * 256, 256), 256)
        high, low = stencil_matrix(
            idx[:, cut] - (base + block * 64 - HW), weight[:, cut], 256, 80
        )
        matrices[block, :128, :] = high
        matrices[block, 128:, :] = low
        cosines, sines = jnp.cos(angle[:, cut]), jnp.sin(angle[:, cut])
        phases[:KIDS, cut] = cosines
        phases[KIDS:, cut] = sines
        return cosines, sines

    wide = lanes((256, 128))

    def do_block(block, tile):
        cosines, sines = fill_matrix(block)
        out = aggregate(interp_product(tile, matrices[block]), cosines, sines)
        for u in range(2):

            def store(half, q, message):
                send[4 * block + 2 * u + half, q] = message

            send_main([o[:, 128 * u : 128 * u + 128] for o in out], store)

    def odd_tile(t):
        return jnp.where(wide < 72, pltpu.roll(own[t], 72, 1), pltpu.roll(own[t + 1], 72, 1))

    fill_matrix(0)
    fill_matrix(2 * count - 2)
    fill_matrix(2 * count - 1)
    do_block(1, odd_tile(0))

    def step(t, carry):
        even = jnp.where(wide < HW, pltpu.roll(own[t - 1], HW, 1), pltpu.roll(own[t], HW, 1))
        do_block(2 * t, even)
        do_block(2 * t + 1, odd_tile(t))
        return carry

    lax.fori_loop(1, count - 1, step, 0)


def halo_lanes(below, above, at):
    return jnp.where(lanes((at[1], 128)) < 32, turn(below[at[0] : at[0] + at[1], :], 32), turn(above[at[0] : at[0] + at[1], :], 32))


def edge_kernel(
    where, ends, below, above, matrix_lo, matrix_hi, phases_lo, phases_hi, send_in, send,
    edge_matrix, edge_phases, first, last, beyond, messages, rest, sems,
):
    base = where[1] * 1152
    lane = lanes()
    for at in range(PAR * KIDS):
        a, i = at // 8, at % 8
        cut = slice(8 * at, 8 * at + 8)
        low_halo = below[8 * a : 8 * a + 8, :]
        high_halo = above[8 * a : 8 * a + 8, :]
        low_own = ends[0, cut, :]
        high_own = ends[2, cut, :]
        first[cut, :] = jnp.where(lane < HW, turn(low_halo, -(16 * i + 8)), turn(low_own, HW))
        last[1, cut, :] = jnp.where(lane < 72, turn(high_own, 72), turn(high_halo, 72 - 16 * i))
        last[0, cut, :] = jnp.where(lane < HW, turn(ends[1, cut, :], HW), turn(high_own, HW))
        edge = jnp.where(lane < 16, turn(low_halo, -16 * i), turn(low_own, 16))
        edge = jnp.where(lane < 24, edge, turn(high_own, 32))
        beyond[cut, :] = jnp.where(lane < 32, edge, turn(high_halo, 32 - 16 * i))

    row = halo_lanes(below, above, (IDX_AT, 8)).astype(jnp.int32) - base
    row = row + jnp.where(lane < 32, 16, 24 - 1144)
    weight = jnp.where(lane < 64, halo_lanes(below, above, (WEIGHT_AT, 8)), 0.0)
    high, low = stencil_matrix(row, weight, 128, 48)
    edge_matrix[:128, :] = high
    edge_matrix[128:, :] = low
    shift = halo_lanes(below, above, (SHIFT_AT, 8))[:KIDS]
    edge_phases[:KIDS, :] = jnp.cos(shift)
    edge_phases[KIDS:, :] = jnp.sin(shift)

    out = aggregate(interp_product(first[...], matrix_lo[0]), phases_lo[:KIDS, :], phases_lo[KIDS:, :])
    for u in range(2):

        def store(half, q, message):
            messages[2 * u + half, q] = message

        send_main([o[:, 128 * u : 128 * u + 128] for o in out], store)

    tiles = []
    for k in range(2):
        cut = slice(256 * k, 256 * k + 256)
        out = aggregate(
            interp_product(last[k], matrix_hi[k]), phases_hi[:KIDS, cut], phases_hi[KIDS:, cut]
        )
        for u in range(2):
            tiles.append([o[:, 128 * u : 128 * u + 128] for o in out])
    tiles.append(
        aggregate(interp_product(beyond[...], edge_matrix[...]), edge_phases[:KIDS, :], edge_phases[KIDS:, :])
    )
    piece = lane // EXTRA
    for e in range(5):
        for i in range(8):
            message = tiles[e][0]
            message = turn(message, -16 * i)
            for p in range(1, PAR):
                message = jnp.where(piece == p, turn(tiles[e][p], 16 * (p - i)), message)
            rest[8 * e + i] = message
    rest[40:] = jnp.zeros((24, 8, 128), F32)
    one = pltpu.make_async_copy(messages, send.at[0:4, 0:4], sems.at[0])
    two = pltpu.make_async_copy(rest, send.at[:, 4], sems.at[1])
    one.start()
    two.start()
    one.wait()
    two.wait()


def translate_kernel(where, lists, received, table, table_rest, below, above, send, sources, factors):
    lane = lanes()
    box = where[0]
    low = lane < MAIN
    for c in range(2):
        at = (REAL_AT, IMAG_AT)[c]
        wide = lanes((TERMS, 128))
        main = pltpu.roll(table[c], (128 - MAIN * (box % 2)) % 128, 1)
        beyond = jnp.where(
            wide < 32,
            turn(below[at : at + TERMS, :], 32),
            turn(above[at : at + TERMS, :], 32),
        )
        extra = jnp.where(box < 32, table_rest[c], beyond)
        extra = pltpu.roll(extra, (MAIN + 128 - EXTRA * (box % 8)) % 128, 1)
        both = jnp.where(wide < MAIN, main, extra)
        for j in range(TERMS):
            factors[c, j] = jnp.broadcast_to(both[j : j + 1, :], (8, 128))

    def unpack(g, carry):
        rest = received[g, 4]
        for q in range(PAR // 2):
            message = received[g, q]
            sources[PAR * g + 2 * q] = jnp.where(low, message, turn(rest, MAIN - EXTRA * (2 * q)))
            sources[PAR * g + 2 * q + 1] = jnp.where(
                low, turn(message, MAIN), turn(rest, MAIN - EXTRA * (2 * q + 1))
            )
        return carry

    lax.fori_loop(0, received.shape[0], unpack, 0, unroll=2)
    flip = sign(128)
    piece = lane // EXTRA
    parents = sources.shape[0]

    def group(g, carry):
        straight = [jnp.zeros((8, 128), F32)] * PAR
        crossed = [jnp.zeros((8, 128), F32)] * PAR
        for j in range(TERMS):
            real, imag = factors[0, j], factors[1, j]
            for i in range(PAR):
                source = sources[lists[j * parents + g * PAR + i]]
                straight[i] = straight[i] + real * source
                crossed[i] = crossed[i] + imag * source
        out = [straight[i] + flip * swapped(crossed[i]) for i in range(PAR)]
        for q in range(PAR // 2):
            send[g, q] = jnp.where(low, out[2 * q], turn(out[2 * q + 1], MAIN))
        rest = turn(out[0], -MAIN)
        for i in range(1, PAR):
            rest = jnp.where(piece == i, turn(out[i], EXTRA * i - MAIN), rest)
        send[g, 4] = rest
        return carry

    lax.fori_loop(0, parents // PAR, group, 0)


def spread_rows(tiles, cosines, sines):
    width = tiles[0].shape[1]
    flip = -sign(width)
    crossed = [flip * swapped(tile) for tile in tiles]
    parts = []
    for s in range(KIDS):
        for p in range(PAR):
            parts.append(tiles[p] * cosines[s : s + 1, :] + crossed[p] * sines[s : s + 1, :])
    return jnp.concatenate(parts, axis=0)


def final_kernel(kids, received, matrices, phases, edge_matrix, edge_phases, out, even, odd, placed, sems):
    lane = lanes()
    low = lane < MAIN
    count = even.shape[0]

    def main_tiles(tile_at):
        tiles = [None] * PAR
        for q in range(PAR // 2):
            first, second = received[2 * tile_at, q], received[2 * tile_at + 1, q]
            tiles[2 * q] = jnp.where(low, first, turn(second, MAIN))
            tiles[2 * q + 1] = jnp.where(low, turn(first, MAIN), second)
        return tiles

    piece = lane // EXTRA

    def extra_tiles(e):
        tiles = []
        for p in range(PAR):
            tile = turn(received[8 * e, 4], -16 * p)
            for i in range(1, 8):
                tile = jnp.where(piece == i, turn(received[8 * e + i, 4], 16 * (i - p)), tile)
            tiles.append(tile)
        return tiles

    def block_of(block, tiles_at):
        left, right = tiles_at
        tiles = [jnp.concatenate([left[p], right[p]], axis=1) for p in range(PAR)]
        cut = pl.ds(block * 256, 256)
        return anterp_product(
            spread_rows(tiles, phases[:KIDS, cut], phases[KIDS:, cut]), matrices[block]
        )

    def step(t, carry):
        first = pl.multiple_of(2 * t, 2)
        even[t] = block_of(first, (main_tiles(4 * t), main_tiles(4 * t + 1)))
        odd[t] = block_of(first + 1, (main_tiles(4 * t + 2), main_tiles(4 * t + 3)))
        return carry

    lax.fori_loop(0, count - 1, step, 0)
    even[count - 1] = block_of(2 * count - 2, (extra_tiles(0), extra_tiles(1)))
    odd[count - 1] = block_of(2 * count - 1, (extra_tiles(2), extra_tiles(3)))
    tiles = [jnp.where(low, tile, 0.0) for tile in extra_tiles(4)]
    beyond = anterp_product(
        spread_rows(tiles, edge_phases[:KIDS, :], edge_phases[KIDS:, :]), edge_matrix[...]
    )

    for at in range(PAR * KIDS):
        cut = slice(8 * at, 8 * at + 8)
        place = kid_rows(kids, at)
        evens = [turn(even[t, cut, :], -HW) for t in range(count)]
        odds = [turn(odd[t, cut, :], 56) for t in range(count)]
        for t in range(count):
            from_even = jnp.where(lane < 120, evens[t], evens[t + 1] if t + 1 < count else 0.0)
            from_odd = jnp.where(lane >= HW, odds[t], odds[t - 1] if t > 0 else 0.0)
            total = from_even + from_odd
            if t == 0:
                total = total + jnp.where(lane < HW, turn(beyond[cut, :], -16), 0.0)
            if t == count - 1:
                total = total + jnp.where(lane >= 120, turn(beyond[cut, :], 96), 0.0)
            placed.at[t][place, :] = total
    copies = [
        pltpu.make_async_copy(placed.at[t], out.at[:, 128 * t : 128 * t + 128], sems.at[t])
        for t in range(count)
    ]
    for copy in copies:
        copy.start()
    for copy in copies:
        copy.wait()


def smem():
    return pl.BlockSpec(memory_space=pltpu.SMEM)


def vmem():
    return pl.BlockSpec(memory_space=pltpu.VMEM)


def any_space():
    return pl.BlockSpec(memory_space=pl.ANY)


def shards(
    child_field, child_of, shift_angle, interp_index, interp_weight, interaction_list, translation
):
    box_index = lax.axis_index("box")
    dir_index = lax.axis_index("dir")
    dirs = lax.axis_size("dir")
    boxes = lax.axis_size("box")
    halves, fields, own_boxes, strip_child = child_field.shape
    strip_par = interp_index.shape[1]
    count = strip_child // 128
    row_count = halves * fields * own_boxes
    shape = jax.ShapeDtypeStruct
    child = child_field.reshape(row_count, strip_child)
    kids = child_of.reshape(-1)
    where = jnp.stack([box_index, dir_index]).astype(jnp.int32)
    last_par = strip_par // 128 - 1

    def edge(block, at):
        index = (0,) * (len(block) - 1) + (at,)
        return pl.BlockSpec(block, lambda i, *_: index)

    both = lambda block, last: [edge(block, 0), edge(block, last)]
    lo_pack, hi_pack = pl.pallas_call(
        pack_kernel,
        grid_spec=pltpu.PrefetchScalarGridSpec(
            num_scalar_prefetch=1,
            grid=(1,),
            in_specs=both((row_count, 128), count - 1)
            + both((STENCIL, 128), last_par)
            + both((STENCIL, 128), last_par)
            + both((KIDS, 128), last_par)
            + both((2, TERMS, 128), last_par),
            out_specs=[pl.BlockSpec((PACK_ROWS, 128), lambda i, *_: (0, 0))] * 2,
        ),
        out_shape=[shape((PACK_ROWS, 128), F32)] * 2,
        name="pack",
    )(
        kids, child, child, interp_index, interp_index, interp_weight, interp_weight,
        shift_angle, shift_angle, translation, translation,
    )
    forward = [(i, i + 1) for i in range(dirs - 1)]
    backward = [(i + 1, i) for i in range(dirs - 1)]
    below = lax.ppermute(hi_pack, "dir", forward)
    above = lax.ppermute(lo_pack, "dir", backward)

    send, matrices, phases, ends = pl.pallas_call(
        inner_kernel,
        in_specs=[smem(), smem(), any_space(), vmem(), vmem(), vmem()],
        out_specs=[vmem()] * 4,
        out_shape=[
            shape((boxes, 5, 8, 128), F32),
            shape((2 * count, 256, 256), BF16),
            shape((8, strip_par), F32),
            shape((3, row_count, 128), F32),
        ],
        scratch_shapes=[pltpu.VMEM((count, row_count, 128), F32)] * 2
        + [pltpu.SemaphoreType.DMA((count,))],
        name="inner",
    )(kids, where, child, interp_index, interp_weight, shift_angle)

    def whole(*block):
        return pl.BlockSpec(block, lambda i, *_: (0,) * len(block))

    send, edge_matrix, edge_phases = pl.pallas_call(
        edge_kernel,
        grid_spec=pltpu.PrefetchScalarGridSpec(
            num_scalar_prefetch=1,
            grid=(1,),
            in_specs=[
                whole(3, row_count, 128),
                whole(PACK_ROWS, 128),
                whole(PACK_ROWS, 128),
                edge((1, 256, 256), 0),
                pl.BlockSpec((2, 256, 256), lambda i, *_: (count - 1, 0, 0)),
                edge((8, 256), 0),
                edge((8, 512), strip_par // 512 - 1),
                any_space(),
            ],
            out_specs=[any_space(), whole(256, 128), whole(8, 128)],
            scratch_shapes=[
                pltpu.VMEM((row_count, 128), F32),
                pltpu.VMEM((2, row_count, 128), F32),
                pltpu.VMEM((row_count, 128), F32),
                pltpu.VMEM((4, 4, 8, 128), F32),
                pltpu.VMEM((boxes, 8, 128), F32),
                pltpu.SemaphoreType.DMA((2,)),
            ],
        ),
        out_shape=[shape(send.shape, F32), shape((256, 128), BF16), shape((8, 128), F32)],
        input_output_aliases={8: 0},
        name="edge",
    )(where, ends, below, above, matrices, matrices, phases, phases, send)

    received = lax.all_to_all(send, "box", split_axis=0, concat_axis=0, tiled=True)
    parents = interaction_list.shape[1]
    answered = pl.pallas_call(
        translate_kernel,
        grid_spec=pltpu.PrefetchScalarGridSpec(
            num_scalar_prefetch=2,
            grid=(1,),
            in_specs=[
                pl.BlockSpec((boxes, 5, 8, 128), lambda i, *_: (0, 0, 0, 0)),
                pl.BlockSpec((2, TERMS, 128), lambda i, w, l: (0, 0, w[0] // 2)),
                pl.BlockSpec(
                    (2, TERMS, 128), lambda i, w, l: (0, 0, jnp.minimum(32 + w[0] // 8, last_par))
                ),
                pl.BlockSpec((PACK_ROWS, 128), lambda i, *_: (0, 0)),
                pl.BlockSpec((PACK_ROWS, 128), lambda i, *_: (0, 0)),
            ],
            out_specs=pl.BlockSpec((boxes, 5, 8, 128), lambda i, *_: (0, 0, 0, 0)),
            scratch_shapes=[
                pltpu.VMEM((parents, 8, 128), F32),
                pltpu.VMEM((2, TERMS, 8, 128), F32),
            ],
        ),
        out_shape=shape((boxes, 5, 8, 128), F32),
        name="translate",
    )(where, interaction_list.reshape(-1), received, translation, translation, below, above)
    incoming = lax.all_to_all(answered, "box", split_axis=0, concat_axis=0, tiled=True)

    out = pl.pallas_call(
        final_kernel,
        in_specs=[smem()] + [vmem()] * 5,
        out_specs=any_space(),
        out_shape=shape((row_count, strip_child), F32),
        scratch_shapes=[pltpu.VMEM((count, row_count, 128), F32)] * 3
        + [pltpu.SemaphoreType.DMA((count,))],
        name="final",
    )(kids, incoming, matrices, phases, edge_matrix, edge_phases)
    return out.reshape(child_field.shape)


def solution(mesh):
    in_specs = (
        P(None, None, "box", "dir"),
        P("box", None),
        P(None, "dir"),
        P(None, "dir"),
        P(None, "dir"),
        P(),
        P(None, None, "dir"),
    )
    out_specs = P(None, None, "box", "dir")
    return jax.shard_map(shards, mesh=mesh, in_specs=in_specs, out_specs=out_specs, check_vma=False)
```

time: 558 us -> 121 us (0.22)
  other arithmetic: 219 us -> 0.64 us
  local copies, waits for them, and re-layouts: 180 us -> 6.08 us
  Pallas kernels: 0 us -> 49.4 us
  matrix products: 47.2 us -> 0 us
  waiting for transfers between devices: 64.5 us -> 20.4 us
  blocking collectives: 0 us -> 26.6 us
  starting transfers between devices: 29.2 us -> 17.1 us
  loops' own time: 11.3 us -> 0 us
    gather x27 -> x0, local copies, waits for them, and re-layouts: 131 us -> none  [add_term(): source = jnp.take(source_field, source_ids, axis=0)]
    add x30 -> x0, other arithmetic: 101 us -> none  [the longest x27 96.2 us: add_term(): carry[1] + op_real * src_imag + op_imag * src_real]
    select_n x54 -> x0, other arithmetic: 97.4 us -> none  [add_term(): source = jnp.take(source_field, source_ids, axis=0)]
    pallas_call x0 -> x5, Pallas kernels: none -> 49.4 us  [the longest x1 25.4 us: shards(): pl.pallas_call(translate_kernel, grid_spec=pltpu.PrefetchScalarGridSpec(n...]
    dot_general x20 -> x0, matrix products: 47.2 us -> none  [the longest x9 21.4 us: interp_block(): jnp.dot(columns, matrices[block_at], precision=lax.Precision.HIGHEST, pre...]
    all_to_all x2 -> x1, waiting for transfers between devices: 56.7 us -> 20.4 us  [shards(): lax.all_to_all(send, 'box', split_axis=0, concat_axis=0, tiled=True)]
    all_to_all x0 -> x1, blocking collectives: none -> 26.6 us  [shards(): lax.all_to_all(answered, 'box', split_axis=0, concat_axis=0, tiled=True)]
    slice x48 -> x0, local copies, waits for them, and re-layouts: 11.9 us -> none  [the longest x9 9.4 us: build_matrix(): weight_block[stencil_at][None, :]]
  transfers between devices with their start and end apart: 6 -> 3, of which waited for: 4 -> 1; matrix products, arithmetic and copies ran while one was open for 7% -> 1% of each run, Pallas kernels for 0% -> 8%
where the time goes in v1:
time: 121 us; the launch traced here: 120 us
  Pallas kernels  49.4 us (41%)
  blocking collectives  26.6 us (22%)
  waiting for transfers between devices  20.4 us (17%)
  starting transfers between devices  17.1 us (14%)
  local copies, waits for them, and re-layouts  6.08 us (5%)
    all_to_all x1, blocking collectives, shards(): lax.all_to_all(answered, 'box', split_axis=0, concat_axis=0, tiled=True)  26.6 us
    pallas_call x1, Pallas kernels, shards(): pl.pallas_call(translate_kernel, grid_spec=pltpu.PrefetchScalarGridSpec(n...  25.4 us
    all_to_all x1, waiting for transfers between devices, shards(): lax.all_to_all(send, 'box', split_axis=0, concat_axis=0, tiled=True)  20.4 us
    pallas_call x1, Pallas kernels, shards(): pl.pallas_call(inner_kernel, in_specs=[smem(), smem(), any_space(), vmem(...  9.22 us
    all_to_all x1, starting transfers between devices, shards(): lax.all_to_all(send, 'box', split_axis=0, concat_axis=0, tiled=True)  9.04 us
    pallas_call x1, Pallas kernels, shards(): pl.pallas_call(final_kernel, in_specs=[smem()] + [vmem()] * 5, out_specs=...  7.97 us
    ppermute x1, starting transfers between devices, shards(): below = lax.ppermute(hi_pack, 'dir', forward)  6.1 us
    unnamed x10, local copies, waits for them, and re-layouts  4.87 us
  transfers between devices with their start and end apart: 3, of which 1 were waited for; matrix products, arithmetic and copies ran while one was open for 1% of the time, Pallas kernels for 8%

profile of v1, /device:TPU:65, one launch (start us, length us, event | category | flops | bytes accessed | tf_op | source)
XLA Modules:
  0.0 120.3 jit_solution(7342686128488852256)
XLA Ops:
  0.0 0.8 copy.14
  0.8 0.6 reshape.12.kids
  1.4 2.4 %copy.15.t_lo.t_hi.table.table_rest = f32[2,27,4608]{2,1,0:T(8,128)} copy(f32[2,27,4608]{2,0,1:T(2,128)} %param.13) | data formatting | bytes 1990656 | tf_op args[6]
  3.8 2.7 %pack.1 = (f32[120,128]{1,0:T(8,128)}, f32[120,128]{1,0:T(8,128)}) custom-call(s32[32]{0:T(128)} %reshape.12.kids, f32[256,1152]{1,0:T(8,128)} %bitcast.4, f32[256,1152]{1,0:T(8,128)} %bitcast.5, s32[6,4608]{1,0:T(8,128)} %idx_hi.1, s32[6,4608]{1,0:T(8,128)} %idx_hi.1, f32[6,4608]{1,0:T(8,128)} %w_hi.1, f32[6,4608]{1,0:T(8,128)} %w_hi.1, f32[4,4608]{1,0:T(4,128)} %a_hi.1, ...), custom_call_target="tpu_custom_call" | custom-call | tf_op jit(solution)/shard_map/pack/pallas_call | solution.py:421
  6.4 6.1 %collective-permute-start = (f32[120,128]{1,0:T(8,128)}, f32[120,128]{1,0:T(8,128)S(1)}, u32[]{:S(2)}, u32[]{:S(2)}) collective-permute-start(f32[120,128]{1,0:T(8,128)} %get-tuple-element.15), channel_id=1, source_target_pairs={{0,1},{1,2},{2,3},{4,5},{5,6},{6,7},{8,9},{9,10},{10,11},{12,13},{... | collective-permute-start | bytes 184328 | tf_op jit(solution)/shard_map/ppermute | solution.py:441
  12.5 1.9 %collective-permute-start.1 = (f32[120,128]{1,0:T(8,128)}, f32[120,128]{1,0:T(8,128)S(1)}, u32[]{:S(2)}, u32[]{:S(2)}) collective-permute-start(f32[120,128]{1,0:T(8,128)} %get-tuple-element.16), channel_id=1, source_target_pairs={{1,0},{2,1},{3,2},{5,4},{6,5},{7,6},{9,8},{10,9},{11,10},{13,12},{... | collective-permute-start | bytes 184328 | tf_op jit(solution)/shard_map/ppermute | solution.py:442
  14.4 0.6 pad_add_fusion.where
  15.1 9.2 %inner.1 = (f32[64,5,8,128]{3,2,1,0:T(8,128)}, bf16[18,256,256]{2,1,0:T(8,128)(2,1)}, f32[8,4608]{1,0:T(8,128)}, f32[3,256,128]{2,1,0:T(8,128)}) custom-call(s32[32]{0:T(128)} %reshape.12.kids, s32[2]{0:T(128)} %pad_add_fusion.where, f32[256,1152]{1,0:T(8,128)} %bitcast.6, s32[6,4608]{1,0:T(8,128)} %idx_hi.1, f32[6,4608]{1,0:T(8,128)} %w_hi.1, f32[4,4608]{1,0:T(4,128)} %a_hi.1), custom_call_target="tpu_custom_call" | custom-call | tf_op jit(solution)/shard_map/inner/pallas_call | solution.py:444
  24.3 0.0 collective-permute-done.below
  24.3 0.0 copy-start.1
  24.3 0.0 collective-permute-done.1.above
  24.3 0.0 copy-start.2
  24.4 0.6 copy-done.1
  24.9 0.0 copy-done.2
  25.0 4.2 %edge.1 = (f32[64,5,8,128]{3,2,1,0:T(8,128)}, bf16[256,128]{1,0:T(8,128)(2,1)}, f32[8,128]{1,0:T(8,128)}) custom-call(s32[2]{0:T(128)} %pad_add_fusion.where, f32[3,256,128]{2,1,0:T(8,128)} %get-tuple-element.14.ends, f32[120,128]{1,0:T(8,128)} %copy-done.1, f32[120,128]{1,0:T(8,128)} %copy-done.2, ...), custom_call_target="tpu_custom_call", output_to_operand_aliasing={{0}: (8, {})} | custom-call | tf_op jit(solution)/shard_map/edge/pallas_call | solution.py:462
  29.1 0.0 copy-start.3
  29.2 9.0 %all-to-all-start = ((f32[64,5,8,128]{3,2,1,0:T(8,128)}), f32[64,5,8,128]{3,2,1,0:T(8,128)S(1)}, u32[]{:S(2)}, u32[]{:S(2)}) async-start(f32[64,5,8,128]{3,2,1,0:T(8,128)} %get-tuple-element.20), calls=%async_computation | async-start | bytes 2621440 | tf_op jit(solution)/shard_map/all_to_all | solution.py:492
  38.2 0.0 copy-done.3
  38.2 0.6 reshape.13.lists
  38.8 20.4 %all-to-all-done.received = f32[64,5,8,128]{3,2,1,0:T(8,128)S(1)} async-done(((f32[64,5,8,128]{3,2,1,0:T(8,128)}), f32[64,5,8,128]{3,2,1,0:T(8,128)S(1)}, u32[]{:S(2)}, u32[]{:S(2)}) %all-to-all-start) | async-done | bytes 1310752 | tf_op jit(solution)/shard_map/all_to_all | solution.py:492
  59.3 0.0 copy-start
  59.3 1.1 copy-done
  60.4 25.4 %translate.1 = f32[64,5,8,128]{3,2,1,0:T(8,128)} custom-call(s32[2]{0:T(128)} %pad_add_fusion.where, s32[13824]{0:T(1024)} %reshape.13.lists, f32[64,5,8,128]{3,2,1,0:T(8,128)} %copy-done, f32[2,27,4608]{2,1,0:T(8,128)} %copy.15.t_lo.t_hi.table.table_rest, f32[2,27,4608]{2,1,0:T(8,128)} %copy.15.t_lo.t_hi.table.table_rest, f32[120,128]{1,0:T(8,128)} %copy-done.1, ...), custom_call_target="tpu_custom_call" | custom-call | tf_op jit(solution)/shard_map/translate/pallas_call | solution.py:494
  85.7 26.6 %all_to_all.10.received = f32[64,5,8,128]{3,2,1,0:T(8,128)} all-to-all(f32[64,5,8,128]{3,2,1,0:T(8,128)} %translate.1), channel_id=1, replica_groups=mesh['box'=64,'dir'=4] {'box'}, dimensions={0} | all-to-all | bytes 2621440 | tf_op jit(solution)/shard_map/all_to_all | solution.py:517
  112.3 8.0 %final.1 = f32[256,1152]{1,0:T(8,128)} custom-call(s32[32]{0:T(128)} %reshape.12.kids, f32[64,5,8,128]{3,2,1,0:T(8,128)} %all_to_all.10.received, bf16[18,256,256]{2,1,0:T(8,128)(2,1)} %get-tuple-element.17.matrix_lo.matrix_hi.matrices, f32[8,4608]{1,0:T(8,128)} %get-tuple-element.18.phases_lo.phases_hi.phases, ...), custom_call_target="tpu_custom_call" | custom-call | tf_op jit(solution)/shard_map/final/pallas_call | solution.py:519
Async XLA Ops:
  6.4 17.9 %collective-permute-start = (f32[120,128]{1,0:T(8,128)}, f32[120,128]{1,0:T(8,128)S(1)}, u32[]{:S(2)}, u32[]{:S(2)}) collective-permute-start(f32[120,128]{1,0:T(8,128)} %get-tuple-element.15), channel_id=1, source_target_pairs={{0,1},{1,2},{2,3},{4,5},{5,6},{6,7},{8,9},{9,10},{10,11},{12,13},{... | collective-permute-start | bytes 184328 | tf_op jit(solution)/shard_map/ppermute | solution.py:441
  12.5 11.8 %collective-permute-start.1 = (f32[120,128]{1,0:T(8,128)}, f32[120,128]{1,0:T(8,128)S(1)}, u32[]{:S(2)}, u32[]{:S(2)}) collective-permute-start(f32[120,128]{1,0:T(8,128)} %get-tuple-element.16), channel_id=1, source_target_pairs={{1,0},{2,1},{3,2},{5,4},{6,5},{7,6},{9,8},{10,9},{11,10},{13,12},{... | collective-permute-start | bytes 184328 | tf_op jit(solution)/shard_map/ppermute | solution.py:442
  24.3 0.6 copy-start.1
  24.3 0.6 copy-start.2
  29.1 9.1 %copy-start.3 = (s32[27,512]{1,0:T(8,128)S(1)}, s32[27,512]{1,0:T(8,128)}, u32[]{:S(2)}) copy-start(s32[27,512]{1,0:T(8,128)} %param.12) | copy-start | bytes 165892
  29.2 30.1 %all-to-all-start = ((f32[64,5,8,128]{3,2,1,0:T(8,128)}), f32[64,5,8,128]{3,2,1,0:T(8,128)S(1)}, u32[]{:S(2)}, u32[]{:S(2)}) async-start(f32[64,5,8,128]{3,2,1,0:T(8,128)} %get-tuple-element.20), calls=%async_computation | async-start | bytes 2621440 | tf_op jit(solution)/shard_map/all_to_all | solution.py:492
  59.3 1.1 copy-start
